TPU v7x, 512 devices: a whole 4x4x16 slice. The times are simulated.
512 devices in a mesh: grp: 64 (over z, y), seq: 8 (over x, core).
Axes of the slice: x: 4, y: 4, z: 16, core: 2. Of those that a mesh axis runs over, the one named last changes fastest.
Arguments:
- tokens: bfloat16 [64, 1024, 2048], P('grp', 'seq'), may hold values from -6 to 6
- seg_ids: int32 [64, 1024], P('grp'), may hold values from 0 to 3, never falling along the last dimension, each value on 1 to 512 neighbouring positions
- deal: int32 [64, 1024], P('grp'), may hold values from 0 to 1023, each once within a row
- page_table: int32 [64, 128], P('grp'), may hold values from 0 to 127, each once within a row
- in_gain: float32 [2048], replicated, may hold values from 0.1 to 1.9
- w_query: bfloat16 [2048, 2048], P('grp', 'seq'), may hold values from -0.125 to 0.125
- key_projection_weight: bfloat16 [2048, 512], P('grp'), may hold values from -0.125 to 0.125
- value_projection_weight: bfloat16 [2048, 512], P('grp'), may hold values from -0.125 to 0.125
- q_gain: float32 [256], replicated, may hold values from 1.25 to 3.75
- key_norm_gain: float32 [256], replicated, may hold values from 0.1 to 1.9
- w_out: bfloat16 [2048, 2048], P('seq', 'grp'), may hold values from -0.125 to 0.125
- post_gain: float32 [2048], replicated, may hold values from 0.1 to 1.9
- final_gain: float32 [2048], replicated, may hold values from 0.1 to 1.9
- embed: bfloat16 [262144, 2048], P(('grp', 'seq')), may hold values from -0.375 to 0.375
Outputs:
- hidden_out: bfloat16 [64, 1024, 2048], P('grp', 'seq')
- kv_cache: bfloat16 [64, 128, 8, 1024], P('grp', 'seq')
- last_norm: float32 [256], replicated
- max_logit: float32 [256], replicated
Inputs may be any that keep to these rules, and one draw needn't show every extreme that they name: `seg_ids`: along each pack the prompt numbers never fall; every one of the 4 prompts occurs, none has more than 512 positions, and one has exactly that many. Each row of deal holds every packed position once. Each row of page_table holds every page of the pack once.
All inputs are finite; a program needn't handle non-finite values.
Results may differ from a plain program's by a relative error of at most 0.015.
The roundings to bfloat16 on the way count: a program that leaves them out, or rounds other values in their place, can miss the bound.
Values may be sent and summed in bfloat16 or wider, within the bound.
A program may use at most 64 MiB of HBM per device.

v0:
```python
import jax
import jax.numpy as jnp
from jax import lax
from jax.sharding import PartitionSpec as P

QUERY_HEADS = 8
KEY_HEADS = 2
PAGE_SLOTS = 8
SEGS = 4
eps = 1e-06
rope_base = 1000000.0
cap_value = 30.0


def rows_scaled(value_rows, scales):
    mean_square = jnp.mean(value_rows * value_rows, axis=-1, keepdims=True)
    return value_rows * lax.rsqrt(mean_square + eps) * scales


def rotate(value_rows, offsets):
    half_width = value_rows.shape[-1] // 2
    frequency = rope_base ** (
        -2.0 * jnp.arange(half_width, dtype=jnp.float32) / value_rows.shape[-1]
    )
    angles = offsets.astype(jnp.float32)[:, None] * frequency[None, :]
    cosine = jnp.cos(angles)[:, None, :]
    sine_table = jnp.sin(angles)[:, None, :]
    lower_half = value_rows[..., :half_width]
    upper_half = value_rows[..., half_width:]
    return jnp.concatenate(
        [
            lower_half * cosine - upper_half * sine_table,
            upper_half * cosine + lower_half * sine_table,
        ],
        axis=-1,
    )


def layout(segment, dealing):
    row_seg = jnp.take(segment, dealing)
    before = jnp.sum((segment[None, :] < row_seg[:, None]).astype(jnp.int32), axis=1)
    return (row_seg, dealing - before)


def attend(query, key_selected, value_selected, row_seg, dealing):
    scores = jnp.einsum("qhd,khd->hqk", query, key_selected, preferred_element_type=jnp.float32)
    allowed = (row_seg[:, None] == row_seg[None, :]) & (dealing[None, :] <= dealing[:, None])
    masked = jnp.where(allowed[None], scores, -1e30)
    row_peak = jnp.max(masked, axis=-1, keepdims=True)
    raw_weights = jnp.where(allowed[None], jnp.exp(masked - row_peak), 0.0)
    row_total = jnp.sum(raw_weights, axis=-1, keepdims=True)
    weights = (raw_weights / row_total).astype(jnp.bfloat16)
    attended = jnp.einsum(
        "hqk,khd->qhd", weights, value_selected, preferred_element_type=jnp.float32
    )
    return attended.astype(jnp.bfloat16).reshape(query.shape[0], -1)


def shards(
    tokens,
    seg_ids,
    deal,
    page_table,
    in_gain,
    w_query,
    key_projection_weight,
    value_projection_weight,
    q_gain,
    key_norm_gain,
    w_out,
    post_gain,
    final_gain,
    embed,
):
    own_tokens = tokens[0]
    rows_dev = own_tokens.shape[0]
    segment = seg_ids[0]
    dealing = deal[0]
    width_of_head = q_gain.shape[0]
    heads_local = w_query.shape[1] // width_of_head
    sequence_index = lax.axis_index("seq")
    own_start = sequence_index * rows_dev
    row_seg, offsets = layout(segment, dealing)
    normed_own = rows_scaled(own_tokens.astype(jnp.float32), in_gain).astype(jnp.bfloat16)
    normed_all = lax.all_gather(normed_own, "seq", axis=0, tiled=True)
    rows_of_pack = normed_all.shape[0]
    key_value_offsets = lax.dynamic_slice_in_dim(offsets, own_start, rows_dev, 0)
    query_full, key_full, value_full, out_full = (
        lax.all_gather(w_query, "grp", axis=0, tiled=True),
        lax.all_gather(key_projection_weight, "grp", axis=0, tiled=True),
        lax.all_gather(value_projection_weight, "grp", axis=0, tiled=True),
        lax.all_gather(w_out, "grp", axis=1, tiled=True),
    )
    query_raw = jnp.dot(normed_all, query_full, preferred_element_type=jnp.float32)
    key_unnormed = jnp.dot(normed_own, key_full, preferred_element_type=jnp.float32)
    value_unnormed = jnp.dot(normed_own, value_full, preferred_element_type=jnp.float32)
    query = rotate(
        rows_scaled(query_raw.reshape(rows_of_pack, heads_local, width_of_head), q_gain), offsets
    ).astype(jnp.bfloat16)
    rows_of_source = normed_own.shape[0]
    key_local_part = rotate(
        rows_scaled(key_unnormed.reshape(rows_of_source, KEY_HEADS, width_of_head), key_norm_gain),
        key_value_offsets,
    ).astype(jnp.bfloat16)
    value_local_part = rows_scaled(
        value_unnormed.reshape(rows_of_source, KEY_HEADS, width_of_head), 1.0
    ).astype(jnp.bfloat16)
    key_local_part = key_local_part.reshape(rows_of_source, KEY_HEADS * width_of_head)
    value_local_part = value_local_part.reshape(rows_of_source, KEY_HEADS * width_of_head)
    key_gathered, value_gathered = (
        lax.all_gather(key_local_part, "seq", axis=0, tiled=True),
        lax.all_gather(value_local_part, "seq", axis=0, tiled=True),
    )
    index_of_head = (sequence_index * heads_local + jnp.arange(heads_local, dtype=jnp.int32)) // (
        QUERY_HEADS // KEY_HEADS
    )
    key_selected = jnp.take(
        key_gathered.reshape(rows_of_pack, KEY_HEADS, width_of_head), index_of_head, axis=1
    )
    value_selected = jnp.take(
        value_gathered.reshape(rows_of_pack, KEY_HEADS, width_of_head), index_of_head, axis=1
    )
    attended = attend(query, key_selected, value_selected, row_seg, dealing)
    partial_out = jnp.dot(attended, out_full, preferred_element_type=jnp.float32)
    summed = lax.psum_scatter(
        partial_out.astype(jnp.bfloat16), "seq", scatter_dimension=0, tiled=True
    ).astype(jnp.float32)
    hidden = (own_tokens.astype(jnp.float32) + rows_scaled(summed, post_gain)).astype(jnp.bfloat16)
    inverse_assignment = jnp.argsort(dealing)
    inverse_page = jnp.argsort(page_table[0])
    own_pages = rows_dev // PAGE_SLOTS
    physical = sequence_index * own_pages + jnp.arange(own_pages, dtype=jnp.int32)
    logical_index = jnp.take(inverse_page, physical)
    packed = logical_index[:, None] * PAGE_SLOTS + jnp.arange(PAGE_SLOTS, dtype=jnp.int32)[None, :]
    source_index = jnp.take(inverse_assignment, packed.reshape(-1))
    stacked_rows = jnp.concatenate([key_gathered, value_gathered], axis=1)
    cache_pages = jnp.take(stacked_rows, source_index, axis=0).reshape(
        own_pages, PAGE_SLOTS, stacked_rows.shape[1]
    )
    last_pos = (
        jnp.sum(
            (segment[None, :] <= jnp.arange(SEGS, dtype=jnp.int32)[:, None]).astype(jnp.int32),
            axis=1,
        )
        - 1
    )
    local_row = jnp.take(inverse_assignment, last_pos) - own_start
    selector = (local_row[:, None] == jnp.arange(rows_dev, dtype=jnp.int32)[None, :]).astype(
        jnp.bfloat16
    )
    group_states = jnp.dot(selector, hidden, preferred_element_type=jnp.float32)
    pack_states = lax.psum(group_states.astype(jnp.bfloat16), "seq")
    states = lax.all_gather(pack_states, "grp", axis=0, tiled=True).astype(jnp.float32)
    last_norm = jnp.sqrt(jnp.mean(states * states, axis=-1))
    final = rows_scaled(states, final_gain).astype(jnp.bfloat16)
    logits = lax.dot_general(
        final, embed, (((1,), (1,)), ((), ())), preferred_element_type=jnp.float32
    )
    shard_max = jnp.max(cap_value * jnp.tanh(logits / cap_value), axis=1)
    max_logit = lax.pmax(shard_max, ("grp", "seq"))
    return (hidden[None], cache_pages[None], last_norm, max_logit)


def solution(mesh):
    return jax.shard_map(
        shards,
        mesh=mesh,
        in_specs=(
            P("grp", "seq", None),
            P("grp", None),
            P("grp", None),
            P("grp", None),
            P(),
            P("grp", "seq"),
            P("grp", None),
            P("grp", None),
            P(),
            P(),
            P("seq", "grp"),
            P(),
            P(),
            P(("grp", "seq"), None),
        ),
        out_specs=(P("grp", "seq", None), P("grp", "seq", None, None), P(), P()),
        check_vma=False,
    )
```

profile of v0, /device:TPU:1, one launch (start us, length us, event | category | flops | bytes accessed | tf_op | source)
XLA Modules:
  0.0 1011.3 jit_solution(3232940448721086610)
XLA Ops:
  9.5 5.7 gather_fusion
  16.3 132.1 %all-gather.18.cloned.1.call-done = bf16[2048,512]{1,0:T(8,128)(2,1)} async-done(((bf16[32,512]{1,0:T(8,128)(2,1)}), bf16[2048,512]{1,0:T(8,128)(2,1)}) %all-gather.18.cloned.1.call-update) | async-done | bytes 2097168 | tf_op jit(solution)/shard_map/all_gather | solution.py:90
  148.5 3.9 copy.40
  152.4 2.5 multiply_reduce_fusion.2
  156.1 132.3 %all-gather.10.cloned.1.call-done = bf16[2048,512]{1,0:T(8,128)(2,1)} async-done(((bf16[32,512]{1,0:T(8,128)(2,1)}), bf16[2048,512]{1,0:T(8,128)(2,1)}) %all-gather.10.cloned.1.call-update) | async-done | bytes 2097168 | tf_op jit(solution)/shard_map/all_gather | solution.py:91
  288.4 4.0 copy.36
  292.4 2.5 multiply_reduce_fusion.3
  298.6 29.0 %all-gather.20.cloned.1.call-done = bf16[1024,512]{1,0:T(8,128)(2,1)} async-done(((bf16[128,512]{1,0:T(8,128)(2,1)}), bf16[1024,512]{1,0:T(8,128)(2,1)}) %all-gather.20.cloned.1.call-update) | async-done | bytes 1048592 | tf_op jit(solution)/shard_map/all_gather | solution.py:111
  327.6 2.2 reshape.529
  329.8 3.3 constant_dynamic-slice_fusion
  333.1 27.5 %all-gather.12.cloned.1.call-done = bf16[1024,512]{1,0:T(8,128)(2,1)} async-done(((bf16[128,512]{1,0:T(8,128)(2,1)}), bf16[1024,512]{1,0:T(8,128)(2,1)}) %all-gather.12.cloned.1.call-update) | async-done | bytes 1048592 | tf_op jit(solution)/shard_map/all_gather | solution.py:112
  360.6 2.2 reshape.527
  362.8 3.3 constant_dynamic-slice_fusion.1
  366.1 126.2 %all-gather.16.cloned.1.call-done = bf16[2048,256]{1,0:T(8,128)(2,1)} async-done(((bf16[32,256]{1,0:T(8,128)(2,1)}), bf16[2048,256]{1,0:T(8,128)(2,1)}) %all-gather.16.cloned.1.call-update) | async-done | bytes 1048592 | tf_op jit(solution)/shard_map/all_gather | solution.py:89
  492.3 48.3 %all-gather.14.cloned.1.call-done = bf16[1024,2048]{1,0:T(8,128)(2,1)} async-done(((bf16[128,2048]{1,0:T(8,128)(2,1)}), bf16[1024,2048]{1,0:T(8,128)(2,1)}) %all-gather.14.cloned.1.call-update) | async-done | bytes 4194320 | tf_op jit(solution)/shard_map/all_gather | solution.py:85
  540.6 3.9 multiply_reduce_fusion.1
  544.7 2.3 fusion.46
  548.0 2.0 copy-done.3
  551.5 121.2 %all-gather.22.cloned.1.call-done = bf16[256,2048]{0,1:T(8,128)(2,1)} async-done(((bf16[256,32]{0,1:T(8,128)(2,1)}), bf16[256,2048]{0,1:T(8,128)(2,1)}) %all-gather.22.cloned.1.call-update) | async-done | bytes 1048592 | tf_op jit(solution)/shard_map/all_gather | solution.py:92
  672.7 7.6 convolution_convert_fusion
  680.4 4.4 sort.35
  684.8 2.5 sort.34
  688.8 40.6 %reduce-scatter.2.cloned.1.call-done = bf16[128,2048]{1,0:T(8,128)(2,1)} async-done(((bf16[1024,2048]{1,0:T(8,128)(2,1)}), bf16[128,2048]{1,0:T(8,128)(2,1)}) %reduce-scatter.2.cloned.1.call-update) | async-done | bytes 524304 | tf_op jit(solution)/shard_map/reduce_scatter | solution.py:125
  730.6 1.5 convolution_convert_fusion.1
  732.1 24.1 %psum.7 = bf16[4,2048]{1,0:T(4,128)(2,1)} all-reduce(bf16[4,2048]{1,0:T(4,128)(2,1)S(1)} %convolution_convert_fusion.1), channel_id=1, replica_groups=mesh['grp'=64,'seq'=8] {'seq'}, use_global_device_ids=true, to_apply=%region_12.14 | all-reduce | flops 8192 | bytes 32768 | tf_op jit(solution)/shard_map/psum | solution.py:152
  757.6 3.2 pad_maximum_fusion
  760.8 2.9 gather_fusion.3
  765.5 121.9 %all-gather.24.cloned.1.call-done = bf16[64,4,2048]{2,1,0:T(4,128)(2,1)} async-done(((bf16[1,4,2048]{2,1,0:T(4,128)(2,1)}), bf16[64,4,2048]{2,1,0:T(4,128)(2,1)}) %all-gather.24.cloned.1.call-update) | async-done | bytes 1048592 | tf_op jit(solution)/shard_map/all_gather | solution.py:153
  887.5 2.5 reshape.630
  890.0 1.8 multiply_reduce_fusion
  892.3 2.4 fusion.10
  894.8 110.0 %pmax.7 = f32[256]{0:T(256)} all-reduce(f32[256]{0:T(256)S(1)} %fusion.10), channel_id=1, replica_groups=mesh['grp'=64,'seq'=8] {'grp','seq'}, use_global_device_ids=true, to_apply=%region_15.17 | all-reduce | flops 256 | bytes 2048 | tf_op jit(solution)/shard_map/pmax | solution.py:160
  (94 shorter events, 17.3 us)
Async XLA Ops:
  7.2 885.2 %copy-start = (bf16[512,2048]{1,0:T(8,128)(2,1)S(1)}, bf16[512,2048]{1,0:T(8,128)(2,1)}, u32[]{:S(2)}) copy-start(bf16[512,2048]{1,0:T(8,128)(2,1)} %param.29) | copy-start | bytes 6291460
  7.2 8.0 copy-start.6
  7.2 8.1 copy-start.1
  7.2 8.6 copy-start.2
  7.2 141.2 %all-gather.18.cloned.1.call-start = ((), (), s32[]{:S(2)}) async-start(), calls=%async_computation.5 | async-start | bytes 2129920 | tf_op jit(solution)/shard_map/all_gather | solution.py:90
  7.9 280.5 %all-gather.10.cloned.1.call-start = ((), (), s32[]{:S(2)}) async-start(), calls=%async_computation.1 | async-start | bytes 2129920 | tf_op jit(solution)/shard_map/all_gather | solution.py:91
  8.7 318.9 %all-gather.20.cloned.1.call-start = ((), (), s32[]{:S(2)}) async-start(), calls=%async_computation.6 | async-start | bytes 1179648 | tf_op jit(solution)/shard_map/all_gather | solution.py:111
  9.4 143.0 %copy-start.7 = (f32[2048]{0:T(1024)S(1)}, f32[2048]{0:T(1024)}, u32[]{:S(2)}) copy-start(f32[2048]{0:T(1024)} %param.20) | copy-start | bytes 24580
  15.2 139.7 %copy-start.9 = (f32[256]{0:T(256)S(1)}, f32[256]{0:T(256)}, u32[]{:S(2)}) copy-start(f32[256]{0:T(256)} %param.25) | copy-start | bytes 3076
  156.0 204.6 %all-gather.12.cloned.1.call-start = ((), (), s32[]{:S(2)}) async-start(), calls=%async_computation.2 | async-start | bytes 1179648 | tf_op jit(solution)/shard_map/all_gather | solution.py:112
  295.9 196.3 %all-gather.16.cloned.1.call-start = ((), (), s32[]{:S(2)}) async-start(), calls=%async_computation.4 | async-start | bytes 1064960 | tf_op jit(solution)/shard_map/all_gather | solution.py:89
  296.5 244.1 %all-gather.14.cloned.1.call-start = ((), (), s32[]{:S(2)}) async-start(), calls=%async_computation.3 | async-start | bytes 4718592 | tf_op jit(solution)/shard_map/all_gather | solution.py:85
  297.6 375.1 %all-gather.22.cloned.1.call-start = ((), (), s32[]{:S(2)}) async-start(), calls=%async_computation.7 | async-start | bytes 1064960 | tf_op jit(solution)/shard_map/all_gather | solution.py:92
  298.3 431.1 %reduce-scatter.2.cloned.1.call-start = ((), (), s32[]{:S(2)}) async-start(), calls=%async_computation.8 | async-start | bytes 4718592 | tf_op jit(solution)/shard_map/reduce_scatter | solution.py:125
  366.1 178.5 %copy-start.10 = (f32[256]{0:T(256)S(1)}, f32[256]{0:T(256)}, u32[]{:S(2)}) copy-start(f32[256]{0:T(256)} %param.24) | copy-start | bytes 3076
  540.6 6.4 copy-start.5
  548.0 2.0 copy-start.3
  680.3 4.5 copy-start.12
  680.3 50.3 %copy-start.8 = (f32[2048]{0:T(1024)S(1)}, f32[2048]{0:T(1024)}, u32[]{:S(2)}) copy-start(f32[2048]{0:T(1024)} %param.27) | copy-start | bytes 24580
  680.3 207.2 %all-gather.24.cloned.1.call-start = ((), (), s32[]{:S(2)}) async-start(), calls=%async_computation.9 | async-start | bytes 1064960 | tf_op jit(solution)/shard_map/all_gather | solution.py:153
  730.6 33.9 %copy-start.4 = (bf16[128,2048]{1,0:T(8,128)(2,1)S(1)}, bf16[128,2048]{1,0:T(8,128)(2,1)}, u32[]{:S(2)}) copy-start(bf16[128,2048]{1,0:T(8,128)(2,1)} %reduce-scatter.2.cloned.1.call-done) | copy-start | bytes 1572868
  763.7 128.7 %copy-start.11 = (f32[2048]{0:T(1024)S(1)}, f32[2048]{0:T(1024)}, u32[]{:S(2)}) copy-start(f32[2048]{0:T(1024)} %param.28) | copy-start | bytes 24580
Sparse Core Ops, SparseCore 0:
  11.0 137.4 all-gather.17
  151.4 136.9 all-gather.9
  291.1 36.4 all-gather.19
  329.6 30.9 all-gather.11
  363.4 128.8 all-gather.15
  494.8 45.7 all-gather.13
  543.6 129.0 all-gather.21
  680.5 48.8 reduce-scatter.1
  756.3 131.0 all-gather.23
where the time goes:
time: 1010 us
  waiting for transfers between devices  782 us (77%)
  blocking collectives  134 us (13%)
  local copies, waits for them, and re-layouts  36.2 us (4%)
  other arithmetic  22.9 us (2%)
  matrix products  21.4 us (2%)
  between operations  14.2 us (1%)
    all_gather x1, waiting for transfers between devices, shards(): lax.all_gather(value_projection_weight, 'grp', axis=0, tiled=True)  132 us
    all_gather x1, waiting for transfers between devices, shards(): lax.all_gather(key_projection_weight, 'grp', axis=0, tiled=True)  132 us
    all_gather x1, waiting for transfers between devices, shards(): lax.all_gather(w_query, 'grp', axis=0, tiled=True)  126 us
    all_gather x1, waiting for transfers between devices, shards(): lax.all_gather(pack_states, 'grp', axis=0, tiled=True).astype(jnp.float32)  122 us
    all_gather x1, waiting for transfers between devices, shards(): lax.all_gather(w_out, 'grp', axis=1, tiled=True)  121 us
    pmax x1, blocking collectives, shards(): max_logit = lax.pmax(shard_max, ('grp', 'seq'))  110 us
    all_gather x1, waiting for transfers between devices, shards(): normed_all = lax.all_gather(normed_own, 'seq', axis=0, tiled=True)  48.3 us
    reduce_scatter x1, waiting for transfers between devices, shards(): lax.psum_scatter(partial_out.astype(jnp.bfloat16), 'seq', scatter_dimensi...  40.6 us
  transfers between devices with their start and end apart: 9, of which 9 were waited for; matrix products, arithmetic and copies ran while one was open for 6% of the time, Pallas kernels for 0%

commit v1 on v0

--- a/solution.py
+++ b/solution.py
@@ -82,7 +82,12 @@
     own_start = sequence_index * rows_dev
     row_seg, offsets = layout(segment, dealing)
     normed_own = rows_scaled(own_tokens.astype(jnp.float32), in_gain).astype(jnp.bfloat16)
-    normed_all = lax.all_gather(normed_own, "seq", axis=0, tiled=True)
+    ring = [normed_own]
+    for hop in range(7):
+        ring.append(lax.ppermute(ring[-1], "seq", [(dev, (dev + 1) % 8) for dev in range(8)]))
+    normed_all = jnp.roll(
+        jnp.concatenate(ring[::-1], axis=0), (lax.axis_index("seq") + 1) * ring[0].shape[0], axis=0
+    )
     rows_of_pack = normed_all.shape[0]
     key_value_offsets = lax.dynamic_slice_in_dim(offsets, own_start, rows_dev, 0)
     query_full, key_full, value_full, out_full = (

time: 1010 us -> 970 us (0.960)
  waiting for transfers between devices: 782 us -> 680 us
  starting transfers between devices: 0.54 us -> 34.4 us
  local copies, waits for them, and re-layouts: 36.2 us -> 56.9 us
    all_gather x1, waiting for transfers between devices: 126 us -> 71 us  [shards(): lax.all_gather(w_query, 'grp', axis=0, tiled=True)]
    all_gather x1 -> x0, waiting for transfers between devices: 48.3 us -> none  [shards(): normed_all = lax.all_gather(normed_own, 'seq', axis=0, tiled=True)]
    ppermute x0 -> x7, starting transfers between devices: none -> 33.9 us  [shards(): lax.ppermute(ring[-1], 'seq', [(dev, (dev + 1) % 8) for dev in range(8)])]
    ppermute x0 -> x7, waiting for transfers between devices: none -> 30.9 us  [shards(): lax.ppermute(ring[-1], 'seq', [(dev, (dev + 1) % 8) for dev in range(8)])]
    all_gather x1, waiting for transfers between devices: 132 us -> 104 us  [shards(): lax.all_gather(value_projection_weight, 'grp', axis=0, tiled=True)]
    unnamed x26 -> x46, local copies, waits for them, and re-layouts: 2.02 us -> 25 us
  transfers between devices with their start and end apart: 9 -> 15, of which waited for: 9 -> 13; matrix products, arithmetic and copies ran while one was open for 6% -> 9% of each run, Pallas kernels for 0% -> 0%
where the time goes in v1:
time: 970 us; the launch traced here: 969 us
  waiting for transfers between devices  680 us (70%)
  blocking collectives  134 us (14%)
  local copies, waits for them, and re-layouts  56.9 us (6%)
  starting transfers between devices  34.4 us (4%)
  other arithmetic  27.7 us (3%)
  matrix products  21.3 us (2%)
  between operations  14.6 us (2%)
    all_gather x1, waiting for transfers between devices, shards(): lax.all_gather(key_projection_weight, 'grp', axis=0, tiled=True)  127 us
    all_gather x1, waiting for transfers between devices, shards(): lax.all_gather(pack_states, 'grp', axis=0, tiled=True).astype(jnp.float32)  122 us
    all_gather x1, waiting for transfers between devices, shards(): lax.all_gather(w_out, 'grp', axis=1, tiled=True)  119 us
    pmax x1, blocking collectives, shards(): max_logit = lax.pmax(shard_max, ('grp', 'seq'))  110 us
    all_gather x1, waiting for transfers between devices, shards(): lax.all_gather(value_projection_weight, 'grp', axis=0, tiled=True)  104 us
    all_gather x1, waiting for transfers between devices, shards(): lax.all_gather(w_query, 'grp', axis=0, tiled=True)  71 us
    reduce_scatter x1, waiting for transfers between devices, shards(): lax.psum_scatter(partial_out.astype(jnp.bfloat16), 'seq', scatter_dimensi...  40.8 us
    ppermute x7, starting transfers between devices, shards(): lax.ppermute(ring[-1], 'seq', [(dev, (dev + 1) % 8) for dev in range(8)])  33.9 us
  transfers between devices with their start and end apart: 15, of which 13 were waited for; matrix products, arithmetic and copies ran while one was open for 9% of the time, Pallas kernels for 0%

profile of v1, /device:TPU:1, one launch (start us, length us, event | category | flops | bytes accessed | tf_op | source)
XLA Modules:
  0.0 969.0 jit_solution(9399103305222079535)
XLA Ops:
  12.0 2.6 collective-permute-start
  16.3 4.5 gather_fusion
  21.7 126.7 %all-gather.15.cloned.1.call-done = bf16[2048,512]{1,0:T(8,128)(2,1)} async-done(((bf16[32,512]{1,0:T(8,128)(2,1)}), bf16[2048,512]{1,0:T(8,128)(2,1)}) %all-gather.15.cloned.1.call-update) | async-done | bytes 2097168 | tf_op jit(solution)/shard_map/all_gather | solution.py:95
  148.5 3.9 copy.40
  152.4 2.5 multiply_reduce_fusion.2
  156.1 10.6 %collective-permute-start.1 = (bf16[128,2048]{1,0:T(8,128)(2,1)S(1)}, bf16[128,2048]{1,0:T(8,128)(2,1)S(1)}, u32[]{:S(2)}, u32[]{:S(2)}) collective-permute-start(bf16[128,2048]{1,0:T(8,128)(2,1)S(1)} %collective-permute-done), channel_id=1, source_target_pairs={{0,1},{1,2},{2,3},{3,4},{4,5},{5,6},{6,7},{7,0},{8,9},{9,10},{10,1... | collective-permute-start | bytes 1572872 | tf_op jit(solution)/shard_map/ppermute | solution.py:87
  166.7 6.1 collective-permute-done.1
  176.1 6.1 collective-permute-done.2
  182.3 2.6 collective-permute-start.3
  184.8 103.5 %all-gather.9.cloned.1.call-done = bf16[2048,512]{1,0:T(8,128)(2,1)} async-done(((bf16[32,512]{1,0:T(8,128)(2,1)}), bf16[2048,512]{1,0:T(8,128)(2,1)}) %all-gather.9.cloned.1.call-update) | async-done | bytes 2097168 | tf_op jit(solution)/shard_map/all_gather | solution.py:96
  288.4 4.0 copy.36
  292.4 2.5 multiply_reduce_fusion.3
  296.0 10.6 %collective-permute-start.4 = (bf16[128,2048]{1,0:T(8,128)(2,1)}, bf16[128,2048]{1,0:T(8,128)(2,1)S(1)}, u32[]{:S(2)}, u32[]{:S(2)}) collective-permute-start(bf16[128,2048]{1,0:T(8,128)(2,1)} %collective-permute-done.3), channel_id=1, source_target_pairs={{0,1},{1,2},{2,3},{3,4},{4,5},{5,6},{6,7},{7,0},{8,9},{9,10},{10,1... | collective-permute-start | bytes 1572872 | tf_op jit(solution)/shard_map/ppermute | solution.py:87
  306.6 6.4 collective-permute-done.4
  316.2 6.1 collective-permute-done.5
  322.4 2.6 collective-permute-start.6
  325.3 6.1 collective-permute-done.6
  354.7 71.0 %all-gather.13.cloned.1.call-done = bf16[2048,256]{1,0:T(8,128)(2,1)} async-done(((bf16[32,256]{1,0:T(8,128)(2,1)}), bf16[2048,256]{1,0:T(8,128)(2,1)}) %all-gather.13.cloned.1.call-update) | async-done | bytes 1048592 | tf_op jit(solution)/shard_map/all_gather | solution.py:94
  425.7 3.8 multiply_reduce_fusion.1
  432.0 33.5 %all-gather.17.cloned.1.call-done = bf16[1024,512]{1,0:T(8,128)(2,1)} async-done(((bf16[128,512]{1,0:T(8,128)(2,1)}), bf16[1024,512]{1,0:T(8,128)(2,1)}) %all-gather.17.cloned.1.call-update) | async-done | bytes 1048592 | tf_op jit(solution)/shard_map/all_gather | solution.py:116
  467.6 30.8 %all-gather.11.cloned.1.call-done = bf16[1024,512]{1,0:T(8,128)(2,1)} async-done(((bf16[128,512]{1,0:T(8,128)(2,1)}), bf16[1024,512]{1,0:T(8,128)(2,1)}) %all-gather.11.cloned.1.call-update) | async-done | bytes 1048592 | tf_op jit(solution)/shard_map/all_gather | solution.py:117
  502.9 3.3 constant_dynamic-slice_fusion.1
  510.7 119.4 %all-gather.19.cloned.1.call-done = bf16[256,2048]{0,1:T(8,128)(2,1)} async-done(((bf16[256,32]{0,1:T(8,128)(2,1)}), bf16[256,2048]{0,1:T(8,128)(2,1)}) %all-gather.19.cloned.1.call-update) | async-done | bytes 1048592 | tf_op jit(solution)/shard_map/all_gather | solution.py:97
  630.1 7.6 convolution_convert_fusion
  637.8 4.4 sort.35
  642.8 2.5 sort.34
  646.0 40.8 %reduce-scatter.2.cloned.1.call-done = bf16[128,2048]{1,0:T(8,128)(2,1)} async-done(((bf16[1024,2048]{1,0:T(8,128)(2,1)}), bf16[128,2048]{1,0:T(8,128)(2,1)}) %reduce-scatter.2.cloned.1.call-update) | async-done | bytes 524304 | tf_op jit(solution)/shard_map/reduce_scatter | solution.py:130
  689.5 24.1 %psum.7 = bf16[4,2048]{1,0:T(4,128)(2,1)} all-reduce(bf16[4,2048]{1,0:T(4,128)(2,1)S(1)} %convolution_convert_fusion.1), channel_id=1, replica_groups=mesh['grp'=64,'seq'=8] {'seq'}, use_global_device_ids=true, to_apply=%region_12.14 | all-reduce | flops 8192 | bytes 32768 | tf_op jit(solution)/shard_map/psum | solution.py:157
  715.0 3.2 pad_maximum_fusion
  718.2 2.9 gather_fusion.3
  723.0 121.9 %all-gather.21.cloned.1.call-done = bf16[64,4,2048]{2,1,0:T(4,128)(2,1)} async-done(((bf16[1,4,2048]{2,1,0:T(4,128)(2,1)}), bf16[64,4,2048]{2,1,0:T(4,128)(2,1)}) %all-gather.21.cloned.1.call-update) | async-done | bytes 1048592 | tf_op jit(solution)/shard_map/all_gather | solution.py:158
  852.2 110.0 %pmax.7 = f32[256]{0:T(256)} all-reduce(f32[256]{0:T(256)S(1)} %fusion.12), channel_id=1, replica_groups=mesh['grp'=64,'seq'=8] {'grp','seq'}, use_global_device_ids=true, to_apply=%region_15.17 | all-reduce | flops 256 | bytes 2048 | tf_op jit(solution)/shard_map/pmax | solution.py:165
  (126 shorter events, 67.6 us)
Async XLA Ops:
  7.2 842.6 %copy-start = (bf16[512,2048]{1,0:T(8,128)(2,1)S(1)}, bf16[512,2048]{1,0:T(8,128)(2,1)}, u32[]{:S(2)}) copy-start(bf16[512,2048]{1,0:T(8,128)(2,1)} %param.29) | copy-start | bytes 6291460
  7.2 9.0 copy-start.1
  7.2 13.6 %copy-start.9 = (s32[1,1024]{1,0:T(1,128)S(1)}, s32[1,1024]{1,0:T(1,128)}, u32[]{:S(2)}) copy-start(s32[1,1024]{1,0:T(1,128)} %param.18) | copy-start | bytes 12292
  7.2 141.2 %all-gather.15.cloned.1.call-start = ((), (), s32[]{:S(2)}) async-start(), calls=%async_computation.4 | async-start | bytes 2129920 | tf_op jit(solution)/shard_map/all_gather | solution.py:95
  7.9 280.5 %all-gather.9.cloned.1.call-start = ((), (), s32[]{:S(2)}) async-start(), calls=%async_computation.1 | async-start | bytes 2129920 | tf_op jit(solution)/shard_map/all_gather | solution.py:96
  8.7 417.0 %all-gather.13.cloned.1.call-start = ((), (), s32[]{:S(2)}) async-start(), calls=%async_computation.3 | async-start | bytes 1064960 | tf_op jit(solution)/shard_map/all_gather | solution.py:94
  12.0 144.1 %collective-permute-start = (bf16[128,2048]{1,0:T(8,128)(2,1)}, bf16[128,2048]{1,0:T(8,128)(2,1)S(1)}, u32[]{:S(2)}, u32[]{:S(2)}) collective-permute-start(bf16[128,2048]{1,0:T(8,128)(2,1)} %fusion.17), channel_id=1, source_target_pairs={{0,1},{1,2},{2,3},{3,4},{4,5},{5,6},{6,7},{7,0},{8,9},{9,10},{10,1... | collective-permute-start | bytes 1572872 | tf_op jit(solution)/shard_map/ppermute | solution.py:87
  14.6 450.8 %all-gather.17.cloned.1.call-start = ((), (), s32[]{:S(2)}) async-start(), calls=%async_computation.5 | async-start | bytes 1179648 | tf_op jit(solution)/shard_map/all_gather | solution.py:116
  16.2 136.2 %copy-start.2 = (bf16[1,128,2048]{2,1,0:T(8,128)(2,1)S(1)}, bf16[1,128,2048]{2,1,0:T(8,128)(2,1)}, u32[]{:S(2)}) copy-start(bf16[1,128,2048]{2,1,0:T(8,128)(2,1)} %param.16) | copy-start | bytes 1572868
  16.2 136.2 %copy-start.10 = (f32[2048]{0:T(1024)S(1)}, f32[2048]{0:T(1024)}, u32[]{:S(2)}) copy-start(f32[2048]{0:T(1024)} %param.20) | copy-start | bytes 24580
  20.8 134.1 %copy-start.12 = (f32[256]{0:T(256)S(1)}, f32[256]{0:T(256)}, u32[]{:S(2)}) copy-start(f32[256]{0:T(256)} %param.25) | copy-start | bytes 3076
  156.0 342.4 %all-gather.11.cloned.1.call-start = ((), (), s32[]{:S(2)}) async-start(), calls=%async_computation.2 | async-start | bytes 1179648 | tf_op jit(solution)/shard_map/all_gather | solution.py:117
  156.1 16.8 %collective-permute-start.1 = (bf16[128,2048]{1,0:T(8,128)(2,1)S(1)}, bf16[128,2048]{1,0:T(8,128)(2,1)S(1)}, u32[]{:S(2)}, u32[]{:S(2)}) collective-permute-start(bf16[128,2048]{1,0:T(8,128)(2,1)S(1)} %collective-permute-done), channel_id=1, source_target_pairs={{0,1},{1,2},{2,3},{3,4},{4,5},{5,6},{6,7},{7,0},{8,9},{9,10},{10,1... | collective-permute-start | bytes 1572872 | tf_op jit(solution)/shard_map/ppermute | solution.py:87
  172.9 0.8 copy-start.4
  173.7 8.6 collective-permute-start.2
  182.3 113.7 %collective-permute-start.3 = (bf16[128,2048]{1,0:T(8,128)(2,1)}, bf16[128,2048]{1,0:T(8,128)(2,1)}, u32[]{:S(2)}, u32[]{:S(2)}) collective-permute-start(bf16[128,2048]{1,0:T(8,128)(2,1)} %collective-permute-done.2), channel_id=1, source_target_pairs={{0,1},{1,2},{2,3},{3,4},{4,5},{5,6},{6,7},{7,0},{8,9},{9,10},{10,1... | collective-permute-start | bytes 1572872 | tf_op jit(solution)/shard_map/ppermute | solution.py:87
  295.9 334.2 %all-gather.19.cloned.1.call-start = ((), (), s32[]{:S(2)}) async-start(), calls=%async_computation.6 | async-start | bytes 1064960 | tf_op jit(solution)/shard_map/all_gather | solution.py:97
  296.0 17.1 %collective-permute-start.4 = (bf16[128,2048]{1,0:T(8,128)(2,1)}, bf16[128,2048]{1,0:T(8,128)(2,1)S(1)}, u32[]{:S(2)}, u32[]{:S(2)}) collective-permute-start(bf16[128,2048]{1,0:T(8,128)(2,1)} %collective-permute-done.3), channel_id=1, source_target_pairs={{0,1},{1,2},{2,3},{3,4},{4,5},{5,6},{6,7},{7,0},{8,9},{9,10},{10,1... | collective-permute-start | bytes 1572872 | tf_op jit(solution)/shard_map/ppermute | solution.py:87
  313.1 0.8 copy-start.6
  313.9 8.5 collective-permute-start.5
  322.4 9.0 collective-permute-start.6
  325.0 361.8 %reduce-scatter.2.cloned.1.call-start = ((), (), s32[]{:S(2)}) async-start(), calls=%async_computation.7 | async-start | bytes 4718592 | tf_op jit(solution)/shard_map/reduce_scatter | solution.py:130
  325.2 15.7 %copy-start.5 = (bf16[128,2048]{1,0:T(8,128)(2,1)S(1)}, bf16[128,2048]{1,0:T(8,128)(2,1)}, u32[]{:S(2)}) copy-start(bf16[128,2048]{1,0:T(8,128)(2,1)} %copy-done.4) | copy-start | bytes 1572868
  335.2 12.2 %copy-start.7 = (bf16[128,2048]{1,0:T(8,128)(2,1)S(1)}, bf16[128,2048]{1,0:T(8,128)(2,1)}, u32[]{:S(2)}) copy-start(bf16[128,2048]{1,0:T(8,128)(2,1)} %copy-done.6) | copy-start | bytes 1572868
  354.7 74.8 %copy-start.13 = (f32[256]{0:T(256)S(1)}, f32[256]{0:T(256)}, u32[]{:S(2)}) copy-start(f32[256]{0:T(256)} %param.24) | copy-start | bytes 3076
  507.2 2.0 copy-start.3
  637.7 5.1 copy-start.15
  637.7 50.3 %copy-start.11 = (f32[2048]{0:T(1024)S(1)}, f32[2048]{0:T(1024)}, u32[]{:S(2)}) copy-start(f32[2048]{0:T(1024)} %param.27) | copy-start | bytes 24580
  637.7 207.1 %all-gather.21.cloned.1.call-start = ((), (), s32[]{:S(2)}) async-start(), calls=%async_computation.8 | async-start | bytes 1064960 | tf_op jit(solution)/shard_map/all_gather | solution.py:158
  688.0 33.9 %copy-start.8 = (bf16[128,2048]{1,0:T(8,128)(2,1)S(1)}, bf16[128,2048]{1,0:T(8,128)(2,1)}, u32[]{:S(2)}) copy-start(bf16[128,2048]{1,0:T(8,128)(2,1)} %reduce-scatter.2.cloned.1.call-done) | copy-start | bytes 1572868
  721.1 128.7 %copy-start.14 = (f32[2048]{0:T(1024)S(1)}, f32[2048]{0:T(1024)}, u32[]{:S(2)}) copy-start(f32[2048]{0:T(1024)} %param.28) | copy-start | bytes 24580
Sparse Core Ops, SparseCore 0:
  11.0 137.4 all-gather.14
  151.4 136.9 all-gather.8
  291.3 134.3 all-gather.12
  428.3 37.1 all-gather.16
  467.5 30.9 all-gather.10
  501.3 128.8 all-gather.18
  637.9 48.8 reduce-scatter.1
  713.7 131.0 all-gather.20
